TPU v7x, 32 devices: a whole 2x2x4 slice. The times are simulated.
32 devices in a mesh: span: 8 (over z, y), plane: 4 (over x, core).
Axes of the slice: x: 2, y: 2, z: 4, core: 2. Of those that a mesh axis runs over, the one named last changes fastest.
Arguments:
- adjoint: float32 [3, 32, 81, 512], P(None, 'span', None, 'plane'), may hold values from -6 to 6
- checkpoints: bfloat16 [8, 2, 32, 81, 512], P(None, None, 'span', None, 'plane'), may hold values from -4 to 4
- checkpoint_step: int32 [3], replicated, may hold values from 0 to 7
- metric: float32 [2, 512], P(None, 'plane'), may hold values from 0.004 to 0.016
- helmholtz_inverse: float32 [32, 81, 81], P('span'), may hold values from -0.08 to 0.8
- wall_element: int32 [1024, 2], replicated, may hold values from 0 to 511
- wall_local: int32 [1024, 2], replicated, may hold values from 0 to 80
- wall_weight: float32 [32, 1024], P('span'), may hold values from 0.7 to 140
Outputs:
- adjoint_next: float32 [3, 32, 81, 512], P(None, 'span', None, 'plane')
- control_gradient: float32 [32, 1024], P('span', 'plane')
All inputs are finite; a program needn't handle non-finite values.
Results may differ from a plain program's by a relative error of at most 0.00065.
Values may be sent and summed in bfloat16 or wider, within the bound.
A program may use at most 128 MiB of HBM per device.

v0:
```python
import jax
import jax.numpy as jnp
import numpy as np
from jax import lax
from jax.sharding import PartitionSpec as P

P_SIZE = 8
NSTEP = 3
HIGHEST = lax.Precision.HIGHEST


def chebyshev_matrix(degree):
    points = np.arange(degree + 1)
    abscissa = np.cos(np.pi * points / degree)
    signed = np.where((points == 0) | (points == degree), 2.0, 1.0) * (-1.0) ** points
    spacing = abscissa[:, None] - abscissa[None, :] + np.eye(degree + 1)
    matrix = signed[:, None] / signed[None, :] / spacing
    return matrix - np.eye(degree + 1) * np.sum(matrix, axis=1)[:, None]


def fourier_table(length):
    row_index = np.arange(length)[:, None]
    column = np.arange(length)[None, :]
    wavenumber = (row_index + 1) // 2
    phase_angle = 2.0 * np.pi * wavenumber * column / length
    parity = row_index % 2
    base_rows = np.where(
        row_index == 0, 1.0, np.where(parity == 1, np.cos(phase_angle), np.sin(phase_angle))
    )
    row_scale = np.where(
        (row_index == 0) | (row_index == length - 1), 1.0 / np.sqrt(length), np.sqrt(2.0 / length)
    )
    return base_rows * row_scale


def transport(field_data, velocity, metric):
    side_nodes = P_SIZE + 1
    matrix = jnp.asarray(chebyshev_matrix(P_SIZE), jnp.float32)
    shaped = field_data.reshape(
        field_data.shape[0], field_data.shape[1], side_nodes, side_nodes, field_data.shape[3]
    )
    first_dir = jnp.einsum("ai,czibe->czabe", matrix, shaped, precision=HIGHEST).reshape(
        field_data.shape
    )
    second_dir = jnp.einsum("bi,czaie->czabe", matrix, shaped, precision=HIGHEST).reshape(
        field_data.shape
    )
    speed_data = velocity.astype(jnp.float32)
    return (
        field_data
        + speed_data[0] * (metric[0] * first_dir)
        + speed_data[1] * (metric[1] * second_dir)
    )


def forward_modes(gathered):
    basis_table = jnp.asarray(fourier_table(gathered.shape[1]), jnp.float32)
    return jnp.einsum("jz,czqe->cjqe", basis_table, gathered, precision=HIGHEST)


def backward_planes(solved):
    basis_table = jnp.asarray(fourier_table(solved.shape[1]), jnp.float32)
    return jnp.einsum("jz,cjqe->czqe", basis_table, solved, precision=HIGHEST)


def solve_modes(inverse_block, coefficients):
    return jnp.einsum("jqr,cjre->cjqe", inverse_block, coefficients, precision=HIGHEST)


def to_plane_layout(point_data):
    return lax.all_to_all(point_data, "span", split_axis=1, concat_axis=3, tiled=True)


def wall_terms(field_one, speed_one, flat_index, inside, wall_count):
    rows = field_one.shape[0]
    values = jnp.take(field_one.reshape(rows, -1), flat_index, axis=1)
    speeds = jnp.take(speed_one.reshape(rows, -1), flat_index, axis=1).astype(jnp.float32)
    product = jnp.where(inside, values * speeds, 0.0).reshape(rows, wall_count, 2)
    return jnp.sum(product, axis=2)


def on_device(
    adjoint,
    checkpoints,
    checkpoint_step,
    metric,
    helmholtz_inverse,
    wall_element,
    wall_local,
    wall_weight,
):
    planes_dev = adjoint.shape[1]
    elems_dev = adjoint.shape[3]
    wall_count = wall_element.shape[0]
    span_count = lax.axis_size("span")
    share = elems_dev // span_count
    all_modes = lax.all_gather(helmholtz_inverse, "span", axis=0, tiled=True)
    offset = lax.axis_index("plane") * elems_dev
    local_element = wall_element - offset
    inside = ((local_element >= 0) & (local_element < elems_dev)).reshape(-1)
    flat_index = (wall_local * elems_dev + jnp.clip(local_element, 0, elems_dev - 1)).reshape(-1)
    velocity = jnp.stack(
        [
            lax.dynamic_index_in_dim(checkpoints, checkpoint_step[s], 0, keepdims=False)
            for s in range(NSTEP)
        ]
    )
    velocity = lax.all_to_all(velocity, "span", split_axis=4, concat_axis=2, tiled=True)
    field = lax.all_to_all(adjoint, "span", split_axis=3, concat_axis=1, tiled=True)
    scale = lax.dynamic_slice_in_dim(metric, lax.axis_index("span") * share, share, 1)
    product = 0.0
    for substep in range(NSTEP):
        advected = transport(field, velocity[substep], scale)
        field = backward_planes(solve_modes(all_modes, forward_modes(advected)))
        product = product + field[1] * velocity[substep, 1].astype(jnp.float32)
    both = to_plane_layout(jnp.concatenate([field, product[None]], axis=0))
    gathered = jnp.take(both[3].reshape(planes_dev, -1), flat_index, axis=1)
    partial_sum = jnp.where(inside, gathered, 0.0).reshape(planes_dev, wall_count, 2).sum(axis=2)
    weighted = wall_weight * partial_sum
    grad_share = lax.psum_scatter(weighted, "plane", scatter_dimension=1, tiled=True)
    square_total = lax.psum(jnp.sum(grad_share * grad_share), ("span", "plane"))
    inverse_rms = lax.rsqrt(square_total / (planes_dev * span_count * wall_count) + 1e-06)
    return (both[:3], grad_share * inverse_rms)


def solution(mesh):
    placed = (
        P(None, "span", None, "plane"),
        P(None, None, "span", None, "plane"),
        P(),
        P(None, "plane"),
        P("span", None, None),
        P(),
        P(),
        P("span", None),
    )
    return jax.shard_map(
        on_device,
        mesh=mesh,
        in_specs=placed,
        out_specs=(P(None, "span", None, "plane"), P("span", "plane")),
        check_vma=False,
    )
```

profile of v0, /device:TPU:0, one launch (start us, length us, event | category | flops | bytes accessed | tf_op | source)
XLA Modules:
  0.0 294.0 jit_solution(10901137514128044966)
XLA Ops:
  9.4 7.3 %all-to-all-start = ((f32[3,4,81,128]{2,1,0,3:T(4,128)}), f32[3,4,81,128]{2,1,0,3:T(4,128)S(1)}, u32[]{:S(2)}, u32[]{:S(2)}) async-start(f32[3,4,81,128]{2,1,0,3:T(4,128)} %copy.182), calls=%async_computation | async-start | bytes 1572864 | tf_op jit(solution)/shard_map/all_to_all | solution.py:109
  28.2 38.0 %all_gather.3 = f32[32,81,81]{2,1,0:T(8,128)S(1)} all-gather(f32[4,81,81]{2,1,0:T(8,128)S(1)} %copy.200), channel_id=1, replica_groups=mesh['span'=8,'plane'=4] {'span'}, dimensions={0}, use_global_device_ids=true | all-gather | bytes 944784 | tf_op jit(solution)/shard_map/all_gather | solution.py:97
  66.1 4.2 %all-to-all-start.1 = ((bf16[3,2,4,81,128]{3,2,1,0,4:T(4,128)(2,1)}), bf16[3,2,4,81,128]{3,2,1,0,4:T(4,128)(2,1)}, u32[]{:S(2)}, u32[]{:S(2)}) async-start(bf16[3,2,4,81,128]{3,2,1,0,4:T(4,128)(2,1)} %pad_maximum_fusion.1), calls=%async_computation.1 | async-start | bytes 1572864 | tf_op jit(solution)/shard_map/all_to_all | solution.py:108
  70.5 4.3 %copy.191 = f32[3,8,4,81,16]{4,2,1,3,0:T(4,128)} copy(f32[3,8,4,81,16]{3,4,1,2,0:T(8,128)S(1)} %bitcast.137) | data formatting | bytes 995328 | tf_op jit(solution)/shard_map/all_to_all | solution.py:109
  76.1 5.8 %copy.197 = f32[3,32,9,9,16]{1,3,4,2,0:T(8,128)} copy(f32[3,32,9,9,16]{4,1,3,2,0:T(8,128)} %bitcast.129) | data formatting | bytes 995328 | tf_op jit(solution)/shard_map/reshape | solution.py:39
  81.9 5.9 %copy.192 = f32[3,32,9,9,16]{1,2,4,3,0:T(8,128)} copy(f32[3,32,9,9,16]{4,1,3,2,0:T(8,128)} %bitcast.130) | data formatting | bytes 995328 | tf_op jit(solution)/shard_map/reshape | solution.py:39
  87.8 5.3 %convolution_bitcast_fusion = f32[3,32,9,9,16]{1,3,4,2,0:T(8,128)S(1)} fusion(f32[9,9,1,1,1]{1,0,4,3,2:T(8,128)S(1)} %copy-done.19, f32[3,32,9,9,16]{1,3,4,2,0:T(8,128)} %copy.197), kind=kOutput, calls=%fused_computation.13 | convolution fusion | flops 13436928 | bytes 995652 | tf_op jit(solution)/shard_map/bi,czaie->czabe/dot_general | solution.py:45
  95.7 5.3 %convolution_bitcast_fusion.1 = f32[3,32,9,9,16]{1,2,4,3,0:T(8,128)S(1)} fusion(f32[9,9,1,1,1]{1,0,4,3,2:T(8,128)S(1)} %copy-done.19, f32[3,32,9,9,16]{1,2,4,3,0:T(8,128)} %copy.192), kind=kOutput, calls=%fused_computation.14 | convolution fusion | flops 13436928 | bytes 995652 | tf_op jit(solution)/shard_map/ai,czibe->czabe/dot_general | solution.py:42
  108.3 2.9 fusion.26
  115.2 4.1 %fusion.11 = f32[3,32,9,9,16]{1,3,4,2,0:T(8,128)S(1)} fusion(f32[9,9,1,1,1]{1,0,4,3,2:T(8,128)S(1)} %copy-done.19, f32[3,32,9,9,16]{1,4,3,2,0:T(8,128)S(1)} %bitcast.127), kind=kOutput, calls=%fused_computation.10 | convolution fusion | flops 13436928 | bytes 995652 | tf_op jit(solution)/shard_map/bi,czaie->czabe/dot_general | solution.py:45
  119.3 5.7 %fusion.8 = f32[3,32,9,9,16]{1,2,4,3,0:T(8,128)} fusion(f32[9,9,1,1,1]{1,0,4,3,2:T(8,128)S(1)} %copy-done.19, f32[3,32,9,9,16]{1,4,3,2,0:T(8,128)S(1)} %bitcast.128), kind=kOutput, calls=%fused_computation.9 | convolution fusion | flops 13436928 | bytes 995652 | tf_op jit(solution)/shard_map/ai,czibe->czabe/dot_general | solution.py:42
  127.9 3.9 %copy.208 = f32[3,32,9,9,16]{1,4,3,2,0:T(8,128)} copy(f32[3,32,9,9,16]{1,2,4,3,0:T(8,128)} %fusion.8) | data formatting | bytes 995328 | tf_op jit(solution)/shard_map/ai,czibe->czabe/transpose | solution.py:42
  131.8 3.3 %copy.209 = f32[3,32,81,16]{2,1,3,0:T(8,128)} copy(f32[3,32,81,16]{1,3,2,0:T(8,128)} %bitcast.134) | data formatting | bytes 995328 | tf_op jit(solution)/shard_map/reshape | solution.py:42
  145.9 4.1 %fusion.17 = f32[3,32,9,9,16]{1,3,4,2,0:T(8,128)S(1)} fusion(f32[9,9,1,1,1]{1,0,4,3,2:T(8,128)S(1)} %copy-done.19, f32[3,32,9,9,16]{1,4,3,2,0:T(8,128)S(1)} %bitcast.125), kind=kOutput, calls=%fused_computation.12 | convolution fusion | flops 13436928 | bytes 995652 | tf_op jit(solution)/shard_map/bi,czaie->czabe/dot_general | solution.py:45
  150.0 5.9 %fusion.14 = f32[3,32,9,9,16]{1,2,4,3,0:T(8,128)} fusion(f32[9,9,1,1,1]{1,0,4,3,2:T(8,128)S(1)} %copy-done.19, f32[3,32,9,9,16]{1,4,3,2,0:T(8,128)S(1)} %bitcast.126), kind=kOutput, calls=%fused_computation.11 | convolution fusion | flops 13436928 | bytes 995652 | tf_op jit(solution)/shard_map/ai,czibe->czabe/dot_general | solution.py:42
  160.0 3.9 %copy.222 = f32[3,32,9,9,16]{1,4,3,2,0:T(8,128)} copy(f32[3,32,9,9,16]{1,2,4,3,0:T(8,128)} %fusion.14) | data formatting | bytes 995328 | tf_op jit(solution)/shard_map/ai,czibe->czabe/transpose | solution.py:42
  163.9 3.3 %copy.223 = f32[3,32,81,16]{2,1,3,0:T(8,128)} copy(f32[3,32,81,16]{1,3,2,0:T(8,128)} %bitcast.136) | data formatting | bytes 995328 | tf_op jit(solution)/shard_map/reshape | solution.py:42
  176.4 5.9 %all-to-all-start.2 = ((f32[4,32,81,16]{2,3,0,1:T(8,128)}), f32[4,32,81,16]{2,3,0,1:T(8,128)S(1)}, u32[]{:S(2)}, u32[]{:S(2)}) async-start(f32[4,32,81,16]{2,3,0,1:T(8,128)} %copy.233), calls=%async_computation.2 | async-start | bytes 2097152 | tf_op jit(solution)/shard_map/all_to_all | solution.py:71
  183.8 18.1 %all-to-all-done.2 = f32[4,32,81,16]{2,3,0,1:T(8,128)S(1)} async-done(((f32[4,32,81,16]{2,3,0,1:T(8,128)}), f32[4,32,81,16]{2,3,0,1:T(8,128)S(1)}, u32[]{:S(2)}, u32[]{:S(2)}) %all-to-all-start.2) | async-done | bytes 663584 | tf_op jit(solution)/shard_map/all_to_all | solution.py:71
  202.1 5.7 %copy.237 = f32[1,4,81,8,16]{1,4,3,2,0:T(8,128)} copy(f32[1,4,81,8,16]{2,4,3,1,0:T(8,128)S(1)} %slice.124) | data formatting | bytes 331776 | tf_op jit(solution)/shard_map/slice | solution.py:117
  207.8 8.0 %gather_fusion = f32[2048,4]{1,0:T(8,128)S(1)} fusion(f32[4,10368]{0,1:T(8,128)} %bitcast.141, s32[2048]{0:T(1024)S(1)} %broadcast_clamp_fusion), kind=kCustom, calls=%fused_computation | custom fusion | bytes 73728 | tf_op jit(solution)/shard_map/jit(_take)/gather | solution.py:117
  215.7 5.8 %select_reduce_fusion = f32[4,1024]{0,1:T(8,128)S(1)} fusion(f32[4,1024,2]{0,2,1:T(2,128)S(1)} %bitcast.149, pred[1024,2]{1,0:T(8,128)(4,1)S(1)} %copy.236, pred[1024,2]{1,0:T(8,128)(4,1)S(1)} %copy.235), kind=kLoop, calls=%fused_computation.32 | loop fusion | flops 20480 | bytes 53248 | tf_op jit(solution)/shard_map/reduce_sum | solution.py:118
  222.9 20.6 %reduce-scatter.4.cloned.1.call-done = f32[256,4]{1,0:T(8,128)} async-done(((f32[1024,4]{1,0:T(8,128)}), f32[256,4]{1,0:T(8,128)}) %reduce-scatter.4.cloned.1.call-update) | async-done | bytes 4112
  246.2 39.5 %psum.7 = f32[]{:T(128)} all-reduce(f32[]{:T(128)} %multiply_reduce_fusion), channel_id=1, replica_groups=mesh['span'=8,'plane'=4] {'span','plane'}, use_global_device_ids=true, to_apply=%region_3.4 | all-reduce | flops 1 | bytes 8 | tf_op jit(solution)/shard_map/psum | solution.py:121
  (117 shorter events, 56.2 us)
Async XLA Ops:
  7.2 19.4 %copy-start = (f32[2,128]{1,0:T(2,128)S(1)}, f32[2,128]{1,0:T(2,128)}, u32[]{:S(2)}) copy-start(f32[2,128]{1,0:T(2,128)} %param.20) | copy-start | bytes 3076
  9.4 56.8 %all-to-all-start = ((f32[3,4,81,128]{2,1,0,3:T(4,128)}), f32[3,4,81,128]{2,1,0,3:T(4,128)S(1)}, u32[]{:S(2)}, u32[]{:S(2)}) async-start(f32[3,4,81,128]{2,1,0,3:T(4,128)} %copy.182), calls=%async_computation | async-start | bytes 1572864 | tf_op jit(solution)/shard_map/all_to_all | solution.py:109
  66.1 37.3 %all-to-all-start.1 = ((bf16[3,2,4,81,128]{3,2,1,0,4:T(4,128)(2,1)}), bf16[3,2,4,81,128]{3,2,1,0,4:T(4,128)(2,1)}, u32[]{:S(2)}, u32[]{:S(2)}) async-start(bf16[3,2,4,81,128]{3,2,1,0,4:T(4,128)(2,1)} %pad_maximum_fusion.1), calls=%async_computation.1 | async-start | bytes 1572864 | tf_op jit(solution)/shard_map/all_to_all | solution.py:108
  81.9 5.9 %copy-start.19 = (f32[9,9,1,1,1]{1,0,4,3,2:T(8,128)S(1)}, f32[9,9,1,1,1]{1,0,4,3,2:T(8,128)}, u32[]{:S(2)}) copy-start(f32[9,9,1,1,1]{1,0,4,3,2:T(8,128)} %constant.60) | copy-start | bytes 976
  103.4 3.8 %copy-start.6 = (f32[3,8,4,81,16]{3,2,1,4,0:T(4,128)S(1)}, f32[3,8,4,81,16]{3,2,1,4,0:T(4,128)}, u32[]{:S(2)}) copy-start(f32[3,8,4,81,16]{3,2,1,4,0:T(4,128)} %copy.184) | copy-start | bytes 1492996
  103.4 3.8 %copy-start.7 = (f32[3,32,81,16]{2,1,3,0:T(8,128)S(1)}, f32[3,32,81,16]{2,1,3,0:T(8,128)}, u32[]{:S(2)}) copy-start(f32[3,32,81,16]{2,1,3,0:T(8,128)} %copy.199) | copy-start | bytes 1492996
  103.4 3.8 %copy-start.16 = (f32[32,32,1,1]{1,0,3,2:T(8,128)S(1)}, f32[32,32,1,1]{1,0,3,2:T(8,128)}, u32[]{:S(2)}) copy-start(f32[32,32,1,1]{1,0,3,2:T(8,128)} %constant.61) | copy-start | bytes 12292
  103.4 3.8 %copy-start.8 = (f32[3,32,81,16]{2,1,3,0:T(8,128)S(1)}, f32[3,32,81,16]{2,1,3,0:T(8,128)}, u32[]{:S(2)}) copy-start(f32[3,32,81,16]{2,1,3,0:T(8,128)} %copy.194) | copy-start | bytes 1492996
  127.9 7.2 %copy-start.12 = (f32[1,2,8,4,81,16]{4,5,2,3,1,0:T(8,128)S(1)}, f32[1,2,8,4,81,16]{4,5,2,3,1,0:T(8,128)}, u32[]{:S(2)}) copy-start(f32[1,2,8,4,81,16]{4,5,2,3,1,0:T(8,128)} %get-tuple-element.15) | copy-start | bytes 995332
  131.8 5.6 %copy-start.2 = (f32[3,32,81,16]{2,1,3,0:T(8,128)S(1)}, f32[3,32,81,16]{2,1,3,0:T(8,128)}, u32[]{:S(2)}) copy-start(f32[3,32,81,16]{2,1,3,0:T(8,128)} %convolution_bitcast_fusion.6) | copy-start | bytes 1492996
  131.8 5.6 %copy-start.9 = (f32[3,32,81,16]{2,1,3,0:T(8,128)S(1)}, f32[3,32,81,16]{2,1,3,0:T(8,128)}, u32[]{:S(2)}) copy-start(f32[3,32,81,16]{2,1,3,0:T(8,128)} %copy.214) | copy-start | bytes 1492996
  137.3 4.6 %copy-start.17 = (f32[32,32,1,1]{1,0,3,2:T(8,128)S(1)}, f32[32,32,1,1]{1,0,3,2:T(8,128)}, u32[]{:S(2)}) copy-start(f32[32,32,1,1]{1,0,3,2:T(8,128)} %constant.61) | copy-start | bytes 12292
  150.0 5.9 %copy-start.5 = (bf16[3,2,4,81,128]{3,4,2,1,0:T(8,128)(2,1)S(1)}, bf16[3,2,4,81,128]{3,4,2,1,0:T(8,128)(2,1)}, u32[]{:S(2)}) copy-start(bf16[3,2,4,81,128]{3,4,2,1,0:T(8,128)(2,1)} %copy-done.4) | copy-start | bytes 1492996
  160.0 7.2 %copy-start.15 = (f32[1,1,8,4,81,16]{4,5,2,3,1,0:T(8,128)S(1)}, f32[1,1,8,4,81,16]{4,5,2,3,1,0:T(8,128)}, u32[]{:S(2)}) copy-start(f32[1,1,8,4,81,16]{4,5,2,3,1,0:T(8,128)} %get-tuple-element.19) | copy-start | bytes 497668
  160.0 7.3 %copy-start.14 = (f32[1,1,8,4,81,16]{4,5,2,3,1,0:T(8,128)S(1)}, f32[1,1,8,4,81,16]{4,5,2,3,1,0:T(8,128)}, u32[]{:S(2)}) copy-start(f32[1,1,8,4,81,16]{4,5,2,3,1,0:T(8,128)} %get-tuple-element.18) | copy-start | bytes 497668
  163.9 3.6 %copy-start.11 = (f32[3,32,81,16]{2,1,3,0:T(8,128)S(1)}, f32[3,32,81,16]{2,1,3,0:T(8,128)}, u32[]{:S(2)}) copy-start(f32[3,32,81,16]{2,1,3,0:T(8,128)} %copy.228) | copy-start | bytes 1492996
  167.3 5.1 %copy-start.18 = (f32[32,32,1,1]{1,0,3,2:T(8,128)S(1)}, f32[32,32,1,1]{1,0,3,2:T(8,128)}, u32[]{:S(2)}) copy-start(f32[32,32,1,1]{1,0,3,2:T(8,128)} %constant.61) | copy-start | bytes 12292
  167.5 6.1 %copy-start.13 = (bf16[3,2,8,4,81,16]{4,3,2,5,1,0:T(4,128)(2,1)S(1)}, bf16[3,2,8,4,81,16]{4,3,2,5,1,0:T(4,128)(2,1)}, u32[]{:S(2)}) copy-start(bf16[3,2,8,4,81,16]{4,3,2,5,1,0:T(4,128)(2,1)} %copy.232) | copy-start | bytes 1492996
  173.5 9.0 %copy-start.21 = (s32[1024,2]{0,1:T(2,128)S(1)}, s32[1024,2]{0,1:T(2,128)}, u32[]{:S(2)}) copy-start(s32[1024,2]{0,1:T(2,128)} %param.22) | copy-start | bytes 24580
  173.6 9.0 %copy-start.22 = (s32[1024,2]{0,1:T(2,128)S(1)}, s32[1024,2]{0,1:T(2,128)}, u32[]{:S(2)}) copy-start(s32[1024,2]{0,1:T(2,128)} %param.23) | copy-start | bytes 24580
  176.4 25.5 %all-to-all-start.2 = ((f32[4,32,81,16]{2,3,0,1:T(8,128)}), f32[4,32,81,16]{2,3,0,1:T(8,128)S(1)}, u32[]{:S(2)}, u32[]{:S(2)}) async-start(f32[4,32,81,16]{2,3,0,1:T(8,128)} %copy.233), calls=%async_computation.2 | async-start | bytes 2097152 | tf_op jit(solution)/shard_map/all_to_all | solution.py:71
  182.3 61.2 %reduce-scatter.4.cloned.1.call-start = ((), (), s32[]{:S(2)}) async-start(), calls=%async_computation.4 | async-start | bytes 655360
  202.1 19.7 %copy-start.20 = (f32[4,1024]{1,0:T(4,128)S(1)}, f32[4,1024]{1,0:T(4,128)}, u32[]{:S(2)}) copy-start(f32[4,1024]{1,0:T(4,128)} %param.24) | copy-start | bytes 49156
  202.1 84.9 %copy-start.1 = (f32[2,128]{1,0:T(2,128)S(1)}, f32[2,128]{1,0:T(2,128)}, u32[]{:S(2)}) copy-start(f32[2,128]{1,0:T(2,128)} %param.20) | copy-start | bytes 3076
  (3 other events, 6.8 us)
Sparse Core Ops, SparseCore 0:
  223.0 20.4 reduce-scatter.3
where the time goes:
time: 299 us; the launch traced here: 294 us
  local copies, waits for them, and re-layouts  79.4 us (27%)
  blocking collectives  77.4 us (26%)
  matrix products  48.6 us (16%)
  waiting for transfers between devices  38.8 us (13%)
  between operations  21.1 us (7%)
  starting transfers between devices  17.7 us (6%)
  other arithmetic  11 us (4%)
    psum x1, blocking collectives, on_device(): square_total = lax.psum(jnp.sum(grad_share * grad_share), ('span', 'plane'))  39.5 us
    all_gather x1, blocking collectives, on_device(): all_modes = lax.all_gather(helmholtz_inverse, 'span', axis=0, tiled=True)  38 us
    unnamed x2, waiting for transfers between devices  20.6 us
    all_to_all x1, waiting for transfers between devices, to_plane_layout(): lax.all_to_all(point_data, 'span', split_axis=1, concat_axis=3, tiled=True)  18.1 us
    dot_general x3, matrix products, transport(): jnp.einsum('ai,czibe->czabe', matrix, shaped, precision=HIGHEST)  16.8 us
    dot_general x3, matrix products, transport(): jnp.einsum('bi,czaie->czabe', matrix, shaped, precision=HIGHEST)  13.5 us
    reshape x2, local copies, waits for them, and re-layouts, transport(): field_data.reshape(field_data.shape[0], field_data.shape[1], side_nodes,...  11.7 us
    transpose x3, local copies, waits for them, and re-layouts, transport(): jnp.einsum('ai,czibe->czabe', matrix, shaped, precision=HIGHEST)  8.53 us
  transfers between devices with their start and end apart: 4, of which 2 were waited for; matrix products, arithmetic and copies ran while one was open for 14% of the time, Pallas kernels for 0%

commit v1 on v0

--- a/solution.py
+++ b/solution.py
@@ -94,7 +94,15 @@
     wall_count = wall_element.shape[0]
     span_count = lax.axis_size("span")
     share = elems_dev // span_count
-    all_modes = lax.all_gather(helmholtz_inverse, "span", axis=0, tiled=True)
+    ways, here, step = (lax.axis_size("span"), lax.axis_index("span"), helmholtz_inverse.shape[0])
+    line, have = (helmholtz_inverse, 1)
+    while have < ways:
+        line = jnp.concatenate(
+            [line, lax.ppermute(line, "span", [(d, (d - have) % ways) for d in range(ways)])],
+            axis=0,
+        )
+        have = 2 * have
+    all_modes = jnp.roll(line, here * step, axis=0)
     offset = lax.axis_index("plane") * elems_dev
     local_element = wall_element - offset
     inside = ((local_element >= 0) & (local_element < elems_dev)).reshape(-1)

time: 299 us -> 321 us (1.074)
  waiting for transfers between devices: 38.8 us -> 83.8 us
  blocking collectives: 77.4 us -> 39.5 us
  starting transfers between devices: 17.7 us -> 29.8 us
  local copies, waits for them, and re-layouts: 79.4 us -> 83.5 us
    ppermute x0 -> x3, waiting for transfers between devices: none -> 39.3 us  [on_device(): lax.ppermute(line, 'span', [(d, (d - have) % ways) for d in range(ways)])]
    all_gather x1 -> x0, blocking collectives: 38 us -> none  [on_device(): all_modes = lax.all_gather(helmholtz_inverse, 'span', axis=0, tiled=True)]
    ppermute x0 -> x3, starting transfers between devices: none -> 13.3 us  [on_device(): lax.ppermute(line, 'span', [(d, (d - have) % ways) for d in range(ways)])]
    all_to_all x1, waiting for transfers between devices: 18.1 us -> 23.9 us  [to_plane_layout(): lax.all_to_all(point_data, 'span', split_axis=1, concat_axis=3, tiled=True)]
    dot_general x3, matrix products: 16.8 us -> 11.6 us  [transport(): jnp.einsum('ai,czibe->czabe', matrix, shaped, precision=HIGHEST)]
    dot_general x3, matrix products: 8.19 us -> 12.5 us  [solve_modes(): jnp.einsum('jqr,cjre->cjqe', inverse_block, coefficients, precision=HIGHEST)]
    unnamed x54 -> x76, local copies, waits for them, and re-layouts: 7.92 us -> 11.7 us
  transfers between devices with their start and end apart: 4 -> 7, of which waited for: 2 -> 5; matrix products, arithmetic and copies ran while one was open for 14% -> 9% of each run, Pallas kernels for 0% -> 0%
where the time goes in v1:
time: 321 us; the launch traced here: 316 us
  waiting for transfers between devices  83.8 us (26%)
  local copies, waits for them, and re-layouts  83.5 us (26%)
  matrix products  46.5 us (14%)
  blocking collectives  39.5 us (12%)
  starting transfers between devices  29.8 us (9%)
  between operations  21.4 us (7%)
  other arithmetic  11 us (3%)
    psum x1, blocking collectives, on_device(): square_total = lax.psum(jnp.sum(grad_share * grad_share), ('span', 'plane'))  39.5 us
    ppermute x3, waiting for transfers between devices, on_device(): lax.ppermute(line, 'span', [(d, (d - have) % ways) for d in range(ways)])  39.3 us
    all_to_all x1, waiting for transfers between devices, to_plane_layout(): lax.all_to_all(point_data, 'span', split_axis=1, concat_axis=3, tiled=True)  23.9 us
    unnamed x2, waiting for transfers between devices  20.6 us
    dot_general x3, matrix products, transport(): jnp.einsum('bi,czaie->czabe', matrix, shaped, precision=HIGHEST)  14.8 us
    ppermute x3, starting transfers between devices, on_device(): lax.ppermute(line, 'span', [(d, (d - have) % ways) for d in range(ways)])  13.3 us
    dot_general x3, matrix products, solve_modes(): jnp.einsum('jqr,cjre->cjqe', inverse_block, coefficients, precision=HIGHEST)  12.5 us
    unnamed x76, local copies, waits for them, and re-layouts  11.7 us
  transfers between devices with their start and end apart: 7, of which 5 were waited for; matrix products, arithmetic and copies ran while one was open for 9% of the time, Pallas kernels for 0%

profile of v1, /device:TPU:0, one launch (start us, length us, event | category | flops | bytes accessed | tf_op | source)
XLA Modules:
  0.0 315.5 jit_solution(7422812488895268272)
XLA Ops:
  9.4 7.3 %all-to-all-start = ((f32[3,4,81,128]{2,1,0,3:T(4,128)}), f32[3,4,81,128]{2,1,0,3:T(4,128)S(1)}, u32[]{:S(2)}, u32[]{:S(2)}) async-start(f32[3,4,81,128]{2,1,0,3:T(4,128)} %copy.193), calls=%async_computation | async-start | bytes 1572864 | tf_op jit(solution)/shard_map/all_to_all | solution.py:117
  17.5 4.7 %collective-permute-start = (f32[4,81,81]{2,1,0:T(8,128)S(1)}, f32[4,81,81]{2,1,0:T(8,128)S(1)}, u32[]{:S(2)}, u32[]{:S(2)}) collective-permute-start(f32[4,81,81]{2,1,0:T(8,128)S(1)} %get-tuple-element.24), channel_id=1, source_target_pairs={{0,28},{4,0},{8,4},{12,8},{16,12},{20,16},{24,20},{28,24},{1,29},{... | collective-permute-start | bytes 314936 | tf_op jit(solution)/shard_map/ppermute | solution.py:101
  33.4 3.7 %collective-permute-start.1 = (f32[8,81,81]{2,1,0:T(8,128)S(1)}, f32[8,81,81]{2,1,0:T(8,128)S(1)}, u32[]{:S(2)}, u32[]{:S(2)}) collective-permute-start(f32[8,81,81]{2,1,0:T(8,128)S(1)} %pad_maximum_fusion.3), channel_id=1, source_target_pairs={{0,24},{4,28},{8,0},{12,4},{16,8},{20,12},{24,16},{28,20},{1,25},{... | collective-permute-start | bytes 629864 | tf_op jit(solution)/shard_map/ppermute | solution.py:101
  38.7 5.9 %collective-permute-done.1 = f32[8,81,81]{2,1,0:T(8,128)S(1)} collective-permute-done((f32[8,81,81]{2,1,0:T(8,128)S(1)}, f32[8,81,81]{2,1,0:T(8,128)S(1)}, u32[]{:S(2)}, u32[]{:S(2)}) %collective-permute-start.1) | collective-permute-done | bytes 209984 | tf_op jit(solution)/shard_map/ppermute | solution.py:101
  44.8 4.9 %collective-permute-start.2 = (f32[16,81,81]{2,0,1:T(8,128)S(1)}, f32[16,81,81]{2,0,1:T(8,128)S(1)}, u32[]{:S(2)}, u32[]{:S(2)}) collective-permute-start(f32[16,81,81]{2,0,1:T(8,128)S(1)} %copy.214), channel_id=1, source_target_pairs={{0,16},{4,20},{8,24},{12,28},{16,0},{20,4},{24,8},{28,12},{1,17},{... | collective-permute-start | bytes 1259720 | tf_op jit(solution)/shard_map/ppermute | solution.py:101
  51.3 5.6 %all-to-all-start.1 = ((bf16[3,2,4,81,128]{3,2,1,0,4:T(4,128)(2,1)}), bf16[3,2,4,81,128]{3,2,1,0,4:T(4,128)(2,1)}, u32[]{:S(2)}, u32[]{:S(2)}) async-start(bf16[3,2,4,81,128]{3,2,1,0,4:T(4,128)(2,1)} %pad_maximum_fusion.1), calls=%async_computation.1 | async-start | bytes 1572864 | tf_op jit(solution)/shard_map/all_to_all | solution.py:116
  56.8 30.6 %collective-permute-done.2 = f32[16,81,81]{2,0,1:T(8,128)S(1)} collective-permute-done((f32[16,81,81]{2,0,1:T(8,128)S(1)}, f32[16,81,81]{2,0,1:T(8,128)S(1)}, u32[]{:S(2)}, u32[]{:S(2)}) %collective-permute-start.2) | collective-permute-done | bytes 419936 | tf_op jit(solution)/shard_map/ppermute | solution.py:101
  91.9 4.2 %copy.202 = f32[3,8,4,81,16]{4,2,1,3,0:T(4,128)} copy(f32[3,8,4,81,16]{3,4,1,2,0:T(8,128)S(1)} %bitcast.137) | data formatting | bytes 995328 | tf_op jit(solution)/shard_map/all_to_all | solution.py:117
  96.1 5.8 %copy.203 = f32[3,32,9,9,16]{1,2,4,3,0:T(8,128)} copy(f32[3,32,9,9,16]{4,1,3,2,0:T(8,128)} %bitcast.129) | data formatting | bytes 995328 | tf_op jit(solution)/shard_map/reshape | solution.py:39
  101.9 4.3 %copy.208 = f32[3,32,9,9,16]{1,3,4,2,0:T(8,128)S(1)} copy(f32[3,32,9,9,16]{4,1,3,2,0:T(8,128)} %bitcast.130) | data formatting | bytes 995328 | tf_op jit(solution)/shard_map/reshape | solution.py:39
  129.7 4.3 %fusion.26 = f32[3,32,81,16]{2,3,0,1:T(8,128)S(1)} fusion(f32[64,81,81]{2,1,0:T(8,128)} %copy_dynamic-update-slice_fusion.1, s32[]{:T(128)S(6)} %select_n.58, f32[3,32,81,16]{2,1,3,0:T(8,128)S(1)} %convolution_bitcast_fusion.7), kind=kOutput, calls=%fused_computation.27 | convolution fusion | flops 120932352 | bytes 2437124 | tf_op jit(solution)/shard_map/jqr,cjre->cjqe/dot_general | solution.py:67
  135.9 4.1 %fusion.8 = f32[3,32,9,9,16]{1,2,4,3,0:T(8,128)S(1)} fusion(f32[9,9,1,1,1]{1,0,4,3,2:T(8,128)S(1)} %copy-done.26, f32[3,32,9,9,16]{1,4,3,2,0:T(8,128)S(1)} %bitcast.127), kind=kOutput, calls=%fused_computation.9 | convolution fusion | flops 13436928 | bytes 995652 | tf_op jit(solution)/shard_map/ai,czibe->czabe/dot_general | solution.py:42
  140.1 5.6 %fusion.11 = f32[3,32,9,9,16]{1,3,4,2,0:T(8,128)} fusion(f32[9,9,1,1,1]{1,0,4,3,2:T(8,128)S(1)} %copy-done.26, f32[3,32,9,9,16]{1,4,3,2,0:T(8,128)S(1)} %bitcast.128), kind=kOutput, calls=%fused_computation.10 | convolution fusion | flops 13436928 | bytes 995652 | tf_op jit(solution)/shard_map/bi,czaie->czabe/dot_general | solution.py:45
  158.0 4.1 %fusion.29 = f32[3,32,81,16]{2,3,0,1:T(8,128)S(1)} fusion(f32[64,81,81]{2,1,0:T(8,128)} %copy_dynamic-update-slice_fusion.1, s32[]{:T(128)S(6)} %select_n.58, f32[3,32,81,16]{2,1,3,0:T(8,128)S(1)} %convolution_bitcast_fusion.5), kind=kOutput, calls=%fused_computation.28 | convolution fusion | flops 120932352 | bytes 2437124 | tf_op jit(solution)/shard_map/jqr,cjre->cjqe/dot_general | solution.py:67
  164.1 4.1 %fusion.14 = f32[3,32,9,9,16]{1,2,4,3,0:T(8,128)S(1)} fusion(f32[9,9,1,1,1]{1,0,4,3,2:T(8,128)S(1)} %copy-done.26, f32[3,32,9,9,16]{1,4,3,2,0:T(8,128)S(1)} %bitcast.125), kind=kOutput, calls=%fused_computation.11 | convolution fusion | flops 13436928 | bytes 995652 | tf_op jit(solution)/shard_map/ai,czibe->czabe/dot_general | solution.py:42
  168.2 5.8 %fusion.17 = f32[3,32,9,9,16]{1,3,4,2,0:T(8,128)} fusion(f32[9,9,1,1,1]{1,0,4,3,2:T(8,128)S(1)} %copy-done.26, f32[3,32,9,9,16]{1,4,3,2,0:T(8,128)S(1)} %bitcast.126), kind=kOutput, calls=%fused_computation.12 | convolution fusion | flops 13436928 | bytes 995652 | tf_op jit(solution)/shard_map/bi,czaie->czabe/dot_general | solution.py:45
  186.5 4.1 %fusion.32 = f32[3,32,81,16]{2,3,0,1:T(8,128)S(1)} fusion(f32[64,81,81]{2,1,0:T(8,128)} %copy_dynamic-update-slice_fusion.1, s32[]{:T(128)S(6)} %select_n.58, f32[3,32,81,16]{2,1,3,0:T(8,128)S(1)} %convolution_bitcast_fusion.3), kind=kOutput, calls=%fused_computation.29 | convolution fusion | flops 120932352 | bytes 2437124 | tf_op jit(solution)/shard_map/jqr,cjre->cjqe/dot_general | solution.py:67
  194.7 3.6 %all-to-all-start.2 = ((f32[4,32,81,16]{2,3,0,1:T(8,128)}), f32[4,32,81,16]{2,3,0,1:T(8,128)S(1)}, u32[]{:S(2)}, u32[]{:S(2)}) async-start(f32[4,32,81,16]{2,3,0,1:T(8,128)} %copy.251), calls=%async_computation.2 | async-start | bytes 2097152 | tf_op jit(solution)/shard_map/all_to_all | solution.py:71
  199.5 23.9 %all-to-all-done.2 = f32[4,32,81,16]{2,3,0,1:T(8,128)S(1)} async-done(((f32[4,32,81,16]{2,3,0,1:T(8,128)}), f32[4,32,81,16]{2,3,0,1:T(8,128)S(1)}, u32[]{:S(2)}, u32[]{:S(2)}) %all-to-all-start.2) | async-done | bytes 663584 | tf_op jit(solution)/shard_map/all_to_all | solution.py:71
  223.6 5.7 %copy.255 = f32[1,4,81,8,16]{1,4,3,2,0:T(8,128)} copy(f32[1,4,81,8,16]{2,4,3,1,0:T(8,128)S(1)} %slice.124) | data formatting | bytes 331776 | tf_op jit(solution)/shard_map/slice | solution.py:125
  229.3 8.0 %gather_fusion = f32[2048,4]{1,0:T(8,128)S(1)} fusion(f32[4,10368]{0,1:T(8,128)} %bitcast.141, s32[2048]{0:T(1024)S(1)} %broadcast_clamp_fusion), kind=kCustom, calls=%fused_computation | custom fusion | bytes 73728 | tf_op jit(solution)/shard_map/jit(_take)/gather | solution.py:125
  237.3 5.8 %select_reduce_fusion = f32[4,1024]{0,1:T(8,128)S(1)} fusion(f32[4,1024,2]{0,2,1:T(2,128)S(1)} %bitcast.149, pred[1024,2]{1,0:T(8,128)(4,1)S(1)} %copy.254, pred[1024,2]{1,0:T(8,128)(4,1)S(1)} %copy.253), kind=kLoop, calls=%fused_computation.35 | loop fusion | flops 20480 | bytes 53248 | tf_op jit(solution)/shard_map/reduce_sum | solution.py:126
  244.5 20.5 %reduce-scatter.4.cloned.1.call-done = f32[256,4]{1,0:T(8,128)} async-done(((f32[1024,4]{1,0:T(8,128)}), f32[256,4]{1,0:T(8,128)}) %reduce-scatter.4.cloned.1.call-update) | async-done | bytes 4112
  267.7 39.5 %psum.7 = f32[]{:T(128)} all-reduce(f32[]{:T(128)} %multiply_reduce_fusion), channel_id=1, replica_groups=mesh['span'=8,'plane'=4] {'span','plane'}, use_global_device_ids=true, to_apply=%region_3.4 | all-reduce | flops 1 | bytes 8 | tf_op jit(solution)/shard_map/psum | solution.py:129
  (148 shorter events, 77.9 us)
Async XLA Ops:
  7.2 30.0 %copy-start = (f32[2,128]{1,0:T(2,128)S(1)}, f32[2,128]{1,0:T(2,128)}, u32[]{:S(2)}) copy-start(f32[2,128]{1,0:T(2,128)} %param.20) | copy-start | bytes 3076
  7.2 9.6 %copy-start.22 = (f32[4,81,81]{2,0,1:T(4,128)S(1)}, f32[4,81,81]{2,0,1:T(4,128)}, u32[]{:S(2)}) copy-start(f32[4,81,81]{2,0,1:T(4,128)} %param.21) | copy-start | bytes 314932
  7.2 15.0 %copy-start.30 = (s32[3]{0:T(128)S(1)}, s32[3]{0:T(128)}, u32[]{:S(2)}) copy-start(s32[3]{0:T(128)} %param.19) | copy-start | bytes 40
  9.4 41.8 %all-to-all-start = ((f32[3,4,81,128]{2,1,0,3:T(4,128)}), f32[3,4,81,128]{2,1,0,3:T(4,128)S(1)}, u32[]{:S(2)}, u32[]{:S(2)}) async-start(f32[3,4,81,128]{2,1,0,3:T(4,128)} %copy.193), calls=%async_computation | async-start | bytes 1572864 | tf_op jit(solution)/shard_map/all_to_all | solution.py:117
  17.5 15.9 %collective-permute-start = (f32[4,81,81]{2,1,0:T(8,128)S(1)}, f32[4,81,81]{2,1,0:T(8,128)S(1)}, u32[]{:S(2)}, u32[]{:S(2)}) collective-permute-start(f32[4,81,81]{2,1,0:T(8,128)S(1)} %get-tuple-element.24), channel_id=1, source_target_pairs={{0,28},{4,0},{8,4},{12,8},{16,12},{20,16},{24,20},{28,24},{1,29},{... | collective-permute-start | bytes 314936 | tf_op jit(solution)/shard_map/ppermute | solution.py:101
  33.4 11.2 %collective-permute-start.1 = (f32[8,81,81]{2,1,0:T(8,128)S(1)}, f32[8,81,81]{2,1,0:T(8,128)S(1)}, u32[]{:S(2)}, u32[]{:S(2)}) collective-permute-start(f32[8,81,81]{2,1,0:T(8,128)S(1)} %pad_maximum_fusion.3), channel_id=1, source_target_pairs={{0,24},{4,28},{8,0},{12,4},{16,8},{20,12},{24,16},{28,20},{1,25},{... | collective-permute-start | bytes 629864 | tf_op jit(solution)/shard_map/ppermute | solution.py:101
  44.8 42.6 %collective-permute-start.2 = (f32[16,81,81]{2,0,1:T(8,128)S(1)}, f32[16,81,81]{2,0,1:T(8,128)S(1)}, u32[]{:S(2)}, u32[]{:S(2)}) collective-permute-start(f32[16,81,81]{2,0,1:T(8,128)S(1)} %copy.214), channel_id=1, source_target_pairs={{0,16},{4,20},{8,24},{12,28},{16,0},{20,4},{24,8},{28,12},{1,17},{... | collective-permute-start | bytes 1259720 | tf_op jit(solution)/shard_map/ppermute | solution.py:101
  51.3 57.5 %all-to-all-start.1 = ((bf16[3,2,4,81,128]{3,2,1,0,4:T(4,128)(2,1)}), bf16[3,2,4,81,128]{3,2,1,0,4:T(4,128)(2,1)}, u32[]{:S(2)}, u32[]{:S(2)}) async-start(bf16[3,2,4,81,128]{3,2,1,0,4:T(4,128)(2,1)} %pad_maximum_fusion.1), calls=%async_computation.1 | async-start | bytes 1572864 | tf_op jit(solution)/shard_map/all_to_all | solution.py:116
  91.9 4.3 %copy-start.9 = (f32[3,4,81,128]{2,3,1,0:T(8,128)}, f32[3,4,81,128]{2,3,1,0:T(8,128)S(1)}, u32[]{:S(2)}) copy-start(f32[3,4,81,128]{2,3,1,0:T(8,128)S(1)} %copy.194) | copy-start | bytes 1492996
  135.0 5.1 %copy-start.5 = (f32[3,32,81,16]{2,1,3,0:T(8,128)}, f32[3,32,81,16]{2,1,3,0:T(8,128)S(1)}, u32[]{:S(2)}) copy-start(f32[3,32,81,16]{2,1,3,0:T(8,128)S(1)} %convolution_bitcast_fusion.6) | copy-start | bytes 1492996
  145.7 5.5 %copy-start.4 = (f32[3,32,9,9,16]{1,3,4,2,0:T(8,128)S(1)}, f32[3,32,9,9,16]{1,3,4,2,0:T(8,128)}, u32[]{:S(2)}) copy-start(f32[3,32,9,9,16]{1,3,4,2,0:T(8,128)} %fusion.11) | copy-start | bytes 1492996
  153.3 3.6 %copy-start.6 = (f32[3,32,81,16]{2,1,3,0:T(8,128)S(1)}, f32[3,32,81,16]{2,1,3,0:T(8,128)}, u32[]{:S(2)}) copy-start(f32[3,32,81,16]{2,1,3,0:T(8,128)} %copy-done.5) | copy-start | bytes 1492996
  153.3 3.6 %copy-start.13 = (f32[3,32,81,16]{2,1,3,0:T(8,128)S(1)}, f32[3,32,81,16]{2,1,3,0:T(8,128)}, u32[]{:S(2)}) copy-start(f32[3,32,81,16]{2,1,3,0:T(8,128)} %copy.227) | copy-start | bytes 1492996
  153.3 3.6 %copy-start.24 = (f32[32,32,1,1]{1,0,3,2:T(8,128)S(1)}, f32[32,32,1,1]{1,0,3,2:T(8,128)}, u32[]{:S(2)}) copy-start(f32[32,32,1,1]{1,0,3,2:T(8,128)} %constant.84) | copy-start | bytes 12292
  163.1 5.1 %copy-start.7 = (f32[3,32,81,16]{2,1,3,0:T(8,128)}, f32[3,32,81,16]{2,1,3,0:T(8,128)S(1)}, u32[]{:S(2)}) copy-start(f32[3,32,81,16]{2,1,3,0:T(8,128)S(1)} %convolution_bitcast_fusion.4) | copy-start | bytes 1492996
  168.2 5.8 %copy-start.11 = (bf16[3,2,4,81,128]{3,4,2,1,0:T(8,128)(2,1)S(1)}, bf16[3,2,4,81,128]{3,4,2,1,0:T(8,128)(2,1)}, u32[]{:S(2)}) copy-start(bf16[3,2,4,81,128]{3,4,2,1,0:T(8,128)(2,1)} %copy-done.10) | copy-start | bytes 1492996
  175.5 5.1 %copy-start.3 = (f32[3,32,9,9,16]{1,3,4,2,0:T(8,128)S(1)}, f32[3,32,9,9,16]{1,3,4,2,0:T(8,128)}, u32[]{:S(2)}) copy-start(f32[3,32,9,9,16]{1,3,4,2,0:T(8,128)} %fusion.17) | copy-start | bytes 1492996
  186.5 5.2 %copy-start.17 = (bf16[3,2,8,4,81,16]{4,3,2,5,1,0:T(4,128)(2,1)S(1)}, bf16[3,2,8,4,81,16]{4,3,2,5,1,0:T(4,128)(2,1)}, u32[]{:S(2)}) copy-start(bf16[3,2,8,4,81,16]{4,3,2,5,1,0:T(4,128)(2,1)} %copy.250) | copy-start | bytes 1492996
  192.8 5.5 %copy-start.28 = (s32[1024,2]{0,1:T(2,128)S(1)}, s32[1024,2]{0,1:T(2,128)}, u32[]{:S(2)}) copy-start(s32[1024,2]{0,1:T(2,128)} %param.22) | copy-start | bytes 24580
  192.8 5.5 %copy-start.29 = (s32[1024,2]{0,1:T(2,128)S(1)}, s32[1024,2]{0,1:T(2,128)}, u32[]{:S(2)}) copy-start(s32[1024,2]{0,1:T(2,128)} %param.23) | copy-start | bytes 24580
  194.7 28.8 %all-to-all-start.2 = ((f32[4,32,81,16]{2,3,0,1:T(8,128)}), f32[4,32,81,16]{2,3,0,1:T(8,128)S(1)}, u32[]{:S(2)}, u32[]{:S(2)}) async-start(f32[4,32,81,16]{2,3,0,1:T(8,128)} %copy.251), calls=%async_computation.2 | async-start | bytes 2097152 | tf_op jit(solution)/shard_map/all_to_all | solution.py:71
  198.3 66.7 %reduce-scatter.4.cloned.1.call-start = ((), (), s32[]{:S(2)}) async-start(), calls=%async_computation.4 | async-start | bytes 655360
  223.6 19.7 %copy-start.27 = (f32[4,1024]{1,0:T(4,128)S(1)}, f32[4,1024]{1,0:T(4,128)}, u32[]{:S(2)}) copy-start(f32[4,1024]{1,0:T(4,128)} %param.24) | copy-start | bytes 49156
  237.3 71.1 %copy-start.1 = (f32[2,128]{1,0:T(2,128)S(1)}, f32[2,128]{1,0:T(2,128)}, u32[]{:S(2)}) copy-start(f32[2,128]{1,0:T(2,128)} %param.20) | copy-start | bytes 3076
  (14 other events, 36.0 us)
Sparse Core Ops, SparseCore 0:
  244.5 20.4 reduce-scatter.3
